TPU v7x, 128 devices: a whole 4x4x4 slice. The times are simulated.
128 devices in a mesh: dp: 4 (over x), clus: 32 (over y, z, core).
Axes of the slice: x: 4, y: 4, z: 4, core: 2. Of those that a mesh axis runs over, the one named last changes fastest.
Arguments:
- embeddings: bfloat16 [65536, 1024], P(('dp', 'clus')), may hold values from -8 to 8
- parents: int32 [65536, 8], P(('dp', 'clus')), may hold values from 0 to 255, all different within a row; in each aligned block of 512 rows (0 to 511, 512 to 1023, ...) at most 32 rows name the same one
- children: int32 [65536, 8], P(('dp', 'clus')), may hold values from 0 to 1
- temper: float32 [256], P('clus'), may hold values from 0.5 to 2
- level_two: bfloat16 [32768, 1024], P('clus'), may hold values from -2 to 2
- level_three: bfloat16 [65536, 1024], P('clus'), may hold values from -0.1875 to 0.1875
Outputs:
- soft_codes: bfloat16 [65536, 1024], P(('dp', 'clus'))
- candidate_scores: float32 [65536, 1024], P(('dp', 'clus'))
- new_centroids: float32 [32768, 1024], P('clus')
- cluster_mass: float32 [32768], P('clus')
Inputs may be any that keep to these rules, and one draw needn't show every extreme that they name: `parents`: each row names 8 different blocks. Among the rows of one device no block is named by more than 32 rows, and in every draw some block is named by exactly 32 rows of one device.
All inputs are finite; a program needn't handle non-finite values.
Results may differ from a plain program's by a relative error of at most 0.0045.
Values may be sent and summed in bfloat16 or wider, within the bound.
A program may use at most 192 MiB of HBM per device.

v0:
```python
import math
import jax
import jax.numpy as jnp
from jax import lax
from jax.sharding import PartitionSpec as P


def local_ranks(block_ids, first_block, block_count):
    length = block_ids.shape[-1]
    group = math.gcd(length, 128)
    groups = length // group
    leading = block_ids.shape[:-1]
    onehot = (
        (block_ids - first_block)[..., None] == jnp.arange(block_count, dtype=jnp.int32)
    ).astype(jnp.bfloat16)
    grouped = onehot.reshape(leading + (groups, group, block_count))
    lower = (jnp.arange(group)[:, None] > jnp.arange(group)[None, :]).astype(jnp.bfloat16)
    within = jnp.einsum("ij,...gjb->...gib", lower, grouped, preferred_element_type=jnp.float32)
    group_sums = jnp.sum(grouped, axis=-2, dtype=jnp.float32)
    earlier = (jnp.arange(groups)[:, None] > jnp.arange(groups)[None, :]).astype(jnp.float32)
    before = jnp.einsum("hg,...gb->...hb", earlier, group_sums, precision=lax.Precision.HIGHEST)
    counted = within + before[..., None, :]
    position = jnp.sum(counted * grouped.astype(jnp.float32), axis=-1).reshape(leading + (length,))
    return (onehot, position)


def slot_table(onehot, position, most_rows):
    length = position.shape[-1]
    rank_hot = (position[..., None] == jnp.arange(most_rows, dtype=jnp.float32)).astype(jnp.float32)
    numbers = jnp.arange(length, dtype=jnp.float32) + 1.0
    located = jnp.einsum(
        "...nb,...nk->...bk",
        onehot.astype(jnp.float32),
        rank_hot * numbers[:, None],
        precision=lax.Precision.HIGHEST,
    )
    located = located.reshape(located.shape[:-2] + (located.shape[-2] * located.shape[-1],))
    return (located + 0.5).astype(jnp.int32) - 1


def body(embeddings, parents, children, temper, level_two, level_three):
    row_count, features = embeddings.shape
    parent_count = parents.shape[1]
    blocks_here = temper.shape[0]
    block_size = level_two.shape[0] // blocks_here
    child_count = level_three.shape[0] // (blocks_here * block_size)
    shard_count = lax.axis_size("clus")
    own_index = lax.axis_index("clus")
    all_blocks = blocks_here * shard_count
    most_rows = 2 * row_count * parent_count // all_blocks
    item_count = row_count * parent_count
    slot_count = blocks_here * most_rows
    flat_blocks = parents.reshape(item_count)
    own_onehot, own_position = local_ranks(flat_blocks, 0, all_blocks)
    global_slot = flat_blocks * most_rows + own_position.astype(jnp.int32)
    own_item = slot_table(own_onehot, own_position, most_rows)
    own_filled = own_item >= 0
    own_safe = jnp.maximum(own_item, 0)
    all_rows, all_parents, all_children = (
        lax.all_gather(embeddings, "clus", axis=0, tiled=True),
        lax.all_gather(parents, "clus", axis=0, tiled=True),
        lax.all_gather(children, "clus", axis=0, tiled=True),
    )
    source_blocks = all_parents.reshape(shard_count, item_count)
    mine_onehot, mine_position = local_ranks(source_blocks, own_index * blocks_here, blocks_here)
    local_table = slot_table(mine_onehot, mine_position, most_rows)
    sources = jnp.arange(shard_count, dtype=jnp.int32)[:, None]
    slot_item = jnp.where(local_table >= 0, sources * item_count + local_table, -1).reshape(-1)
    filled = slot_item >= 0
    safe_item = jnp.maximum(slot_item, 0)
    slot_rows = jnp.where(filled[:, None], jnp.take(all_rows, safe_item // parent_count, axis=0), 0)
    slot_child = jnp.where(filled, all_children.reshape(-1)[safe_item], -1)
    slot_rows = slot_rows.reshape(shard_count, blocks_here, most_rows, features)
    slot_child = slot_child.reshape(shard_count, blocks_here, most_rows)
    centroids = level_two.reshape(blocks_here, block_size, features)
    scores = jnp.einsum("sbmd,bcd->sbmc", slot_rows, centroids, preferred_element_type=jnp.float32)
    scores = scores * temper[None, :, None, None]
    third = level_three.reshape(blocks_here, child_count, block_size, features)
    deeper = jnp.zeros(scores.shape, jnp.float32)
    for child in range(child_count):
        product = jnp.einsum(
            "sbmd,bcd->sbmc", slot_rows, third[:, child], preferred_element_type=jnp.float32
        )
        deeper = jnp.where((slot_child == child)[..., None], product, deeper)
    back_scores, back_deeper = (
        lax.all_to_all(scores, "clus", split_axis=0, concat_axis=0, tiled=True),
        lax.all_to_all(deeper, "clus", split_axis=0, concat_axis=0, tiled=True),
    )
    item_scores = back_scores.reshape(all_blocks * most_rows, block_size)[global_slot].reshape(
        row_count, parent_count * block_size
    )
    item_deeper = back_deeper.reshape(all_blocks * most_rows, block_size)[global_slot].reshape(
        row_count, parent_count, block_size
    )
    top = jnp.max(item_scores, axis=1, keepdims=True)
    weights = jnp.exp(item_scores - top)
    total = jnp.sum(weights, axis=1, keepdims=True)
    probs = weights / total
    soft_codes = probs.astype(jnp.bfloat16)
    mass = probs.reshape(row_count, parent_count, block_size).sum(axis=2)
    candidate_scores = (parent_count * mass[:, :, None] * item_deeper).reshape(
        row_count, parent_count * block_size
    )
    code_items = probs.reshape(item_count, block_size)
    send_codes = jnp.where(own_filled[:, None], code_items[own_safe], 0.0)
    owner_codes = lax.all_to_all(
        send_codes.reshape(shard_count, slot_count, block_size),
        "clus",
        split_axis=0,
        concat_axis=0,
        tiled=True,
    )
    owner_codes = owner_codes.reshape(shard_count, blocks_here, most_rows, block_size)
    code_high = owner_codes.astype(jnp.bfloat16)
    code_low = (owner_codes - code_high.astype(jnp.float32)).astype(jnp.bfloat16)
    code_pair = jnp.concatenate([code_high, code_low], axis=-1)
    pair_sums = jnp.einsum(
        "sbmc,sbmd->bcd", code_pair, slot_rows, preferred_element_type=jnp.float32
    )
    partial_sums = pair_sums[:, :block_size] + pair_sums[:, block_size:]
    partial_mass = jnp.sum(owner_codes, axis=(0, 2))
    weighted, cluster_mass = lax.psum((partial_sums, partial_mass), "dp")
    cluster_mass = cluster_mass.reshape(blocks_here * block_size)
    new_centroids = (
        weighted.reshape(blocks_here * block_size, features)
        / jnp.maximum(cluster_mass, 1.0)[:, None]
    )
    return (soft_codes, candidate_scores, new_centroids, cluster_mass)


def solution(mesh):
    in_specs = (
        P(("dp", "clus"), None),
        P(("dp", "clus"), None),
        P(("dp", "clus"), None),
        P("clus"),
        P("clus", None),
        P("clus", None),
    )
    out_specs = (P(("dp", "clus"), None), P(("dp", "clus"), None), P("clus", None), P("clus"))
    return jax.shard_map(body, mesh=mesh, in_specs=in_specs, out_specs=out_specs, check_vma=False)
```

profile of v0, /device:TPU:1, one launch (start us, length us, event | category | flops | bytes accessed | tf_op | source)
XLA Modules:
  0.0 820.3 jit_solution(16947258658350363316)
XLA Ops:
  7.9 28.2 %all_gather.9 = s32[16384,8]{0,1:T(8,128)S(1)} all-gather(s32[512,8]{0,1:T(8,128)} %param.7), channel_id=1, replica_groups=mesh['dp'=4,'clus'=32] {'clus'}, dimensions={0}, use_global_device_ids=true | all-gather | bytes 540672 | tf_op jit(solution)/shard_map/all_gather | solution.py:61
  36.1 5.2 copy.63
  41.3 6.4 sub.61
  47.7 7.6 sub.60
  60.5 9.0 %fusion.34 = s32[32,8,32]{2,1,0:T(8,128)S(1)} fusion(f32[4096]{0:T(1024)S(1)} %iota_add_fusion, f32[32,4096]{1,0:T(8,128)S(1)} %bitcast.88, s32[32,4096]{1,0:T(8,128)S(1)} %copy-done.5), kind=kOutput, calls=%fused_computation.55 | convolution fusion | flops 412114944 | bytes 1097728 | tf_op jit(solution)/shard_map/...nb,...nk->...bk/dot_general | solution.py:31
  69.6 25.6 %all_gather.11 = s32[16384,8]{0,1:T(8,128)S(1)} all-gather(s32[512,8]{0,1:T(8,128)S(1)} %copy-done.7), channel_id=1, replica_groups=mesh['dp'=4,'clus'=32] {'clus'}, dimensions={0}, use_global_device_ids=true | all-gather | bytes 540672 | tf_op jit(solution)/shard_map/all_gather | solution.py:62
  95.2 5.4 copy.73
  100.6 6.7 reshape.338
  107.5 45.5 %gather_fusion.2 = s32[8192]{0:T(1024)S(1)} fusion(s32[131072]{0:T(1024)S(1)} %reshape.338, s32[8192]{0:T(1024)S(1)} %broadcast_clamp_fusion.1), kind=kCustom, calls=%fused_computation.2 | custom fusion | bytes 98304 | tf_op jit(solution)/shard_map/gather | solution.py:72
  153.7 240.2 %gather_fusion = bf16[8192,1024]{1,0:T(8,128)(2,1)} fusion(bf16[16384,1024]{1,0:T(8,128)(2,1)} %all-gather.2.cloned.1.call-done, s32[8192]{0:T(1024)S(1)} %broadcast_clamp_fusion.2), kind=kCustom, calls=%fused_computation | custom fusion | bytes 33587200 | tf_op jit(solution)/shard_map/jit(_take)/gather | solution.py:71
  393.9 21.6 %multiply_bitcast_fusion = f32[32,8,32,128]{3,0,2,1:T(8,128)S(1)} fusion(f32[8]{0:T(128)S(1)} %copy-done.10, bf16[8,128,1024,1]{2,1,3,0:T(8,128)(2,1)S(1)} %bitcast.79, bf16[32,8,32,1024]{3,2,1,0:T(8,128)(2,1)} %bitcast.80, pred[32,8,32]{0,2,1:T(8,128)(4,1)S(1)} %copy.68, pred[32,8,32]{0,2,1:T(8,128)(4,1)S(1)} %copy.67), kind=kOutput, calls=%fused_computation.31 | convolution fusion | flops 2165309440 | bytes 23085088 | tf_op jit(solution)/shard_map/sbmd,bcd->sbmc/dot_general | solution.py:76
  415.6 4.4 copy.70
  420.0 89.5 %all-to-all-start = ((f32[32,8,32,128]{3,2,1,0:T(8,128)}), f32[32,8,32,128]{3,2,1,0:T(8,128)}, u32[]{:S(2)}, u32[]{:S(2)}) async-start(f32[32,8,32,128]{3,2,1,0:T(8,128)} %copy.70), calls=%async_computation | async-start | bytes 8388608 | tf_op jit(solution)/shard_map/all_to_all | solution.py:86
  515.2 46.3 %all-to-all-done = f32[32,8,32,128]{3,2,1,0:T(8,128)} async-done(((f32[32,8,32,128]{3,2,1,0:T(8,128)}), f32[32,8,32,128]{3,2,1,0:T(8,128)}, u32[]{:S(2)}, u32[]{:S(2)}) %all-to-all-start) | async-done | bytes 4194336 | tf_op jit(solution)/shard_map/all_to_all | solution.py:86
  561.5 13.0 %gather_fusion.1 = f32[4096,128]{1,0:T(8,128)S(1)} fusion(f32[8192,128]{1,0:T(8,128)} %bitcast.11, s32[4096]{0:T(1024)S(1)} %broadcast_clamp_fusion.3), kind=kCustom, calls=%fused_computation.1 | custom fusion | bytes 4210688 | tf_op jit(solution)/shard_map/gather | solution.py:89
  577.6 3.1 fusion.61
  580.7 28.0 %gather_fusion.4 = f32[8192,128]{1,0:T(8,128)} fusion(f32[4096,128]{1,0:T(8,128)S(1)} %get-tuple-element.7, s32[8192]{0:T(1024)S(1)} %broadcast_clamp_fusion), kind=kCustom, calls=%fused_computation.4 | custom fusion | bytes 8421376 | tf_op jit(solution)/shard_map/gather | solution.py:105
  608.6 5.2 broadcast_select_fusion
  613.9 7.5 all-to-all-start.2
  621.4 21.8 %fusion.21 = f32[8,32,32,128]{3,1,2,0:T(8,128)S(1)} fusion(bf16[8,2,128,1024]{3,2,1,0:T(8,128)(2,1)} %bitcast.97, bf16[32,8,32,1024]{3,2,1,0:T(8,128)(2,1)} %bitcast.81, pred[32,8,32]{0,2,1:T(8,128)(4,1)S(1)} %copy.68, pred[32,8,32]{0,2,1:T(8,128)(4,1)S(1)} %copy.67), kind=kOutput, calls=%fused_computation.41 | convolution fusion | flops 2164260864 | bytes 23085056 | tf_op jit(solution)/shard_map/sbmd,bcd->sbmc/dot_general | solution.py:81
  643.2 17.8 %fusion.12 = f32[32,8,32,128]{3,0,2,1:T(8,128)S(1)} fusion(f32[8,32,32,128]{3,1,2,0:T(8,128)S(1)} %fusion.21, bf16[8,2,128,1024]{3,2,1,0:T(8,128)(2,1)S(1)} %bitcast.98, pred[32,8,32]{0,2,1:T(8,128)(4,1)S(1)} %copy.76, pred[32,8,32]{0,2,1:T(8,128)(4,1)S(1)} %copy.74, bf16[32,8,32,1024]{3,2,1,0:T(8,128)(2,1)} %bitcast.82, pred[32,8,32]{0,2,1:T(8,128)(4,1)S(1)} %copy.68, ...), kind=kOutput, calls=%fused_computation.25 | convolution fusion | flops 2166358016 | bytes 27394048 | tf_op jit(solution)/shard_map/sbmd,bcd->sbmc/dot_general | solution.py:81
  661.0 4.4 copy.78
  665.5 7.8 all-to-all-done.2
  673.3 7.1 all-to-all-start.1
  680.4 4.6 copy.82
  685.8 22.2 %fusion.18 = f32[8,256,1024]{2,1,0:T(8,128)S(1)} fusion(bf16[32,8,32,128]{3,0,2,1:T(8,128)(2,1)S(1)} %get-tuple-element.4, bf16[32,8,32,128]{3,0,2,1:T(8,128)(2,1)S(1)} %get-tuple-element.5, bf16[32,8,32,1024]{3,2,1,0:T(8,128)(2,1)} %bitcast.83, pred[32,8,32]{0,2,1:T(8,128)(4,1)S(1)} %copy.68, pred[32,8,32]{0,2,1:T(8,128)(4,1)S(1)} %copy.67), kind=kOutput, calls=%fused_computation.37 | convolution fusion | flops 4320133120 | bytes 29376512 | tf_op jit(solution)/shard_map/sbmc,sbmd->bcd/dot_general | solution.py:117
  714.0 18.4 %all-to-all-done.1 = f32[32,8,32,128]{3,2,1,0:T(8,128)} async-done(((f32[32,8,32,128]{3,2,1,0:T(8,128)}), f32[32,8,32,128]{3,2,1,0:T(8,128)}, u32[]{:S(2)}, u32[]{:S(2)}) %all-to-all-start.1) | async-done | bytes 4194336 | tf_op jit(solution)/shard_map/all_to_all | solution.py:87
  732.5 16.5 %gather_fusion.3 = f32[4096,128]{1,0:T(8,128)} fusion(f32[8192,128]{1,0:T(8,128)} %bitcast.26, s32[4096]{0:T(1024)S(1)} %broadcast_clamp_fusion.3), kind=kCustom, calls=%fused_computation.3 | custom fusion | bytes 4210688 | tf_op jit(solution)/shard_map/gather | solution.py:92
  752.6 4.4 bitcast_multiply_fusion
  759.5 12.3 %psum.15 = f32[1024]{0:T(1024)S(1)} all-reduce(f32[1024]{0:T(1024)S(1)} %bitcast.95), channel_id=1, replica_groups=mesh['dp'=4,'clus'=32] {'dp'}, use_global_device_ids=true, to_apply=%region_12.13 | all-reduce | flops 1024 | bytes 8192 | tf_op jit(solution)/shard_map/psum | solution.py:122
  771.8 36.5 %all-reduce.2.cloned.1.call-done = f32[1024,1024]{1,0:T(8,128)} async-done(((f32[1024,1024]{1,0:T(8,128)}), f32[1024,1024]{1,0:T(8,128)}) %all-reduce.2.cloned.1.call-update) | async-done | bytes 4194320 | tf_op jit(solution)/shard_map/psum | solution.py:122
  808.3 4.7 broadcast_divide_fusion
  (88 shorter events, 28.2 us)
Async XLA Ops:
  7.2 386.8 %copy-start = (bf16[1024,1024]{1,0:T(8,128)(2,1)S(1)}, bf16[1024,1024]{1,0:T(8,128)(2,1)}, u32[]{:S(2)}) copy-start(bf16[1024,1024]{1,0:T(8,128)(2,1)} %param.10) | copy-start | bytes 6291460
  7.2 146.5 %all-gather.2.cloned.1.call-start = ((), (), s32[]{:S(2)}) async-start(), calls=%async_computation.3 | async-start | bytes 34603008 | tf_op jit(solution)/shard_map/all_gather | solution.py:60
  57.2 3.2 copy-start.5
  60.4 9.2 %copy-start.7 = (s32[512,8]{0,1:T(8,128)S(1)}, s32[512,8]{0,1:T(8,128)}, u32[]{:S(2)}) copy-start(s32[512,8]{0,1:T(8,128)} %param.8) | copy-start | bytes 49156
  153.7 240.2 %copy-start.10 = (f32[8]{0:T(128)S(1)}, f32[8]{0:T(128)}, u32[]{:S(2)}) copy-start(f32[8]{0:T(128)} %param.9) | copy-start | bytes 100
  420.0 89.6 %copy-start.6 = (s32[512,8]{0,1:T(8,128)S(1)}, s32[512,8]{0,1:T(8,128)}, u32[]{:S(2)}) copy-start(s32[512,8]{0,1:T(8,128)} %param.7) | copy-start | bytes 49156
  420.0 141.5 %all-to-all-start = ((f32[32,8,32,128]{3,2,1,0:T(8,128)}), f32[32,8,32,128]{3,2,1,0:T(8,128)}, u32[]{:S(2)}, u32[]{:S(2)}) async-start(f32[32,8,32,128]{3,2,1,0:T(8,128)} %copy.70), calls=%async_computation | async-start | bytes 8388608 | tf_op jit(solution)/shard_map/all_to_all | solution.py:86
  574.5 3.0 copy-start.2
  613.9 59.4 %all-to-all-start.2 = ((f32[32,256,128]{2,1,0:T(8,128)}), f32[32,256,128]{2,1,0:T(8,128)}, u32[]{:S(2)}, u32[]{:S(2)}) async-start(f32[32,256,128]{2,1,0:T(8,128)} %broadcast_select_fusion), calls=%async_computation.2 | async-start | bytes 8388608 | tf_op jit(solution)/shard_map/all_to_all | solution.py:106
  621.4 21.8 %copy-start.9 = (bf16[2048,1024]{1,0:T(8,128)(2,1)S(1)}, bf16[2048,1024]{1,0:T(8,128)(2,1)}, u32[]{:S(2)}) copy-start(bf16[2048,1024]{1,0:T(8,128)(2,1)} %param.11) | copy-start | bytes 12582916
  673.3 59.2 %all-to-all-start.1 = ((f32[32,8,32,128]{3,2,1,0:T(8,128)}), f32[32,8,32,128]{3,2,1,0:T(8,128)}, u32[]{:S(2)}, u32[]{:S(2)}) async-start(f32[32,8,32,128]{3,2,1,0:T(8,128)} %copy.78), calls=%async_computation.1 | async-start | bytes 8388608 | tf_op jit(solution)/shard_map/all_to_all | solution.py:87
  680.4 127.9 %all-reduce.2.cloned.1.call-start = ((), (), s32[]{:S(2)}) async-start(), calls=%async_computation.4 | async-start | bytes 8388608 | tf_op jit(solution)/shard_map/psum | solution.py:122
  710.9 1.6 copy-start.3
  749.0 3.6 copy-start.4
  771.8 41.2 %copy-start.8 = (f32[1024]{0:T(1024)}, f32[1024]{0:T(1024)S(1)}, u32[]{:S(2)}) copy-start(f32[1024]{0:T(1024)S(1)} %psum.15) | copy-start | bytes 12292
  771.8 41.2 %copy-start.1 = (bf16[1024,1024]{1,0:T(8,128)(2,1)S(1)}, bf16[1024,1024]{1,0:T(8,128)(2,1)}, u32[]{:S(2)}) copy-start(bf16[1024,1024]{1,0:T(8,128)(2,1)} %param.10) | copy-start | bytes 6291460
Sparse Core Ops, SparseCore 0:
  10.3 119.2 all-gather.1
  711.1 97.1 all-reduce.1
where the time goes:
time: 832 us; the launch traced here: 820 us
  local copies, waits for them, and re-layouts  398 us (48%)
  waiting for transfers between devices  110 us (13%)
  starting transfers between devices  104 us (12%)
  matrix products  98.9 us (12%)
  blocking collectives  66.1 us (8%)
  other arithmetic  28.1 us (3%)
  between operations  15.1 us (2%)
    gather x1, local copies, waits for them, and re-layouts, body(): jnp.take(all_rows, safe_item // parent_count, axis=0)  240 us
    all_to_all x1, starting transfers between devices, body(): lax.all_to_all(scores, 'clus', split_axis=0, concat_axis=0, tiled=True)  89.5 us
    all_to_all x1, waiting for transfers between devices, body(): lax.all_to_all(scores, 'clus', split_axis=0, concat_axis=0, tiled=True)  46.3 us
    gather x2, local copies, waits for them, and re-layouts, body(): slot_child = jnp.where(filled, all_children.reshape(-1)[safe_item], -1)  45.6 us
    dot_general x2, matrix products, body(): jnp.einsum('sbmd,bcd->sbmc', slot_rows, third[:, child], preferred_elemen...  39.6 us
    psum x1, waiting for transfers between devices, body(): weighted, cluster_mass = lax.psum((partial_sums, partial_mass), 'dp')  36.5 us
    all_gather x1, blocking collectives, body(): lax.all_gather(parents, 'clus', axis=0, tiled=True)  28.2 us
    gather x1, local copies, waits for them, and re-layouts, body(): send_codes = jnp.where(own_filled[:, None], code_items[own_safe], 0.0)  28 us
  transfers between devices with their start and end apart: 5, of which 4 were waited for; matrix products, arithmetic and copies ran while one was open for 24% of the time, Pallas kernels for 0%

commit v1 on v0

--- a/solution.py
+++ b/solution.py
@@ -3,6 +3,11 @@
 import jax.numpy as jnp
 from jax import lax
 from jax.sharding import PartitionSpec as P
+
+
+def all_by_exchange(block, axis, dim):
+    repeated = jnp.stack([block] * lax.axis_size(axis))
+    return jnp.concatenate(lax.all_to_all(repeated, axis, 0, 0), axis=dim)
 
 
 def local_ranks(block_ids, first_block, block_count):
@@ -58,7 +63,7 @@
     own_safe = jnp.maximum(own_item, 0)
     all_rows, all_parents, all_children = (
         lax.all_gather(embeddings, "clus", axis=0, tiled=True),
-        lax.all_gather(parents, "clus", axis=0, tiled=True),
+        all_by_exchange(parents, "clus", 0),
         lax.all_gather(children, "clus", axis=0, tiled=True),
     )
     source_blocks = all_parents.reshape(shard_count, item_count)

time: 832 us -> 813 us (0.977)
  blocking collectives: 66.1 us -> 41.5 us
  starting transfers between devices: 104 us -> 113 us
    all_gather x1 -> x0, blocking collectives: 28.2 us -> none  [body(): lax.all_gather(parents, 'clus', axis=0, tiled=True)]
    sub x3, local copies, waits for them, and re-layouts: 19.2 us -> 6.98 us  [local_ranks(): block_ids - first_block]
    all_to_all x0 -> x1, starting transfers between devices: none -> 9.65 us  [all_by_exchange(): return jnp.concatenate(lax.all_to_all(repeated, axis, 0, 0), axis=dim)]
  transfers between devices with their start and end apart: 5 -> 6, of which waited for: 4 -> 4; matrix products, arithmetic and copies ran while one was open for 24% -> 25% of each run, Pallas kernels for 0% -> 0%
where the time goes in v1:
time: 813 us; the launch traced here: 801 us
  local copies, waits for them, and re-layouts  391 us (48%)
  starting transfers between devices  113 us (14%)
  waiting for transfers between devices  110 us (14%)
  matrix products  101 us (12%)
  blocking collectives  41.5 us (5%)
  other arithmetic  30 us (4%)
  between operations  14.8 us (2%)
    gather x1, local copies, waits for them, and re-layouts, body(): jnp.take(all_rows, safe_item // parent_count, axis=0)  240 us
    all_to_all x1, starting transfers between devices, body(): lax.all_to_all(scores, 'clus', split_axis=0, concat_axis=0, tiled=True)  88.7 us
    all_to_all x1, waiting for transfers between devices, body(): lax.all_to_all(scores, 'clus', split_axis=0, concat_axis=0, tiled=True)  46.5 us
    gather x2, local copies, waits for them, and re-layouts, body(): slot_child = jnp.where(filled, all_children.reshape(-1)[safe_item], -1)  45.6 us
    dot_general x2, matrix products, body(): jnp.einsum('sbmd,bcd->sbmc', slot_rows, third[:, child], preferred_elemen...  39.6 us
    psum x1, waiting for transfers between devices, body(): weighted, cluster_mass = lax.psum((partial_sums, partial_mass), 'dp')  36.4 us
    all_gather x1, blocking collectives, body(): lax.all_gather(children, 'clus', axis=0, tiled=True)  29.1 us
    gather x1, local copies, waits for them, and re-layouts, body(): send_codes = jnp.where(own_filled[:, None], code_items[own_safe], 0.0)  28 us
  transfers between devices with their start and end apart: 6, of which 4 were waited for; matrix products, arithmetic and copies ran while one was open for 25% of the time, Pallas kernels for 0%

profile of v1, /device:TPU:1, one launch (start us, length us, event | category | flops | bytes accessed | tf_op | source)
XLA Modules:
  0.0 800.8 jit_solution(14424262593980489277)
XLA Ops:
  9.5 9.6 %all-to-all-start = ((s32[32,512,8]{1,2,0:T(8,128)}), s32[32,512,8]{1,2,0:T(8,128)}, u32[]{:S(2)}, u32[]{:S(2)}) async-start(s32[32,512,8]{1,2,0:T(8,128)} %stack.2), calls=%async_computation | async-start | bytes 1048576 | tf_op jit(solution)/shard_map/all_to_all | solution.py:10
  19.3 29.1 %all_gather.7 = s32[16384,8]{0,1:T(8,128)S(1)} all-gather(s32[512,8]{0,1:T(8,128)} %param.8), channel_id=1, replica_groups=mesh['dp'=4,'clus'=32] {'clus'}, dimensions={0}, use_global_device_ids=true | all-gather | bytes 540672 | tf_op jit(solution)/shard_map/all_gather | solution.py:67
  48.4 5.2 copy.79
  53.6 7.2 reshape.339
  71.0 3.8 fusion.6
  78.2 10.1 %fusion.34 = s32[32,8,32]{2,1,0:T(8,128)S(1)} fusion(f32[4096]{0:T(1024)S(1)} %iota_add_fusion, f32[32,4096]{1,0:T(8,128)} %bitcast.92, s32[32,4096]{1,0:T(8,128)S(1)} %copy.68), kind=kOutput, calls=%fused_computation.55 | convolution fusion | flops 412114944 | bytes 1097728 | tf_op jit(solution)/shard_map/...nb,...nk->...bk/dot_general | solution.py:36
  88.6 45.5 %gather_fusion.2 = s32[8192]{0:T(1024)S(1)} fusion(s32[131072]{0:T(1024)S(1)} %reshape.339, s32[8192]{0:T(1024)S(1)} %broadcast_clamp_fusion.1), kind=kCustom, calls=%fused_computation.2 | custom fusion | bytes 98304 | tf_op jit(solution)/shard_map/gather | solution.py:77
  134.8 240.2 %gather_fusion = bf16[8192,1024]{1,0:T(8,128)(2,1)} fusion(bf16[16384,1024]{1,0:T(8,128)(2,1)} %all-gather.2.cloned.1.call-done, s32[8192]{0:T(1024)S(1)} %broadcast_clamp_fusion.2), kind=kCustom, calls=%fused_computation | custom fusion | bytes 33587200 | tf_op jit(solution)/shard_map/jit(_take)/gather | solution.py:76
  375.0 22.0 %multiply_bitcast_fusion = f32[32,8,32,128]{3,0,2,1:T(8,128)S(1)} fusion(f32[8]{0:T(128)S(1)} %copy-done.8, bf16[8,128,1024,1]{2,1,3,0:T(8,128)(2,1)S(1)} %bitcast.81, bf16[32,8,32,1024]{3,2,1,0:T(8,128)(2,1)} %bitcast.84, pred[32,8,32]{0,2,1:T(8,128)(4,1)S(1)} %copy.74, pred[32,8,32]{0,2,1:T(8,128)(4,1)S(1)} %copy.73), kind=kOutput, calls=%fused_computation.31 | convolution fusion | flops 2165309440 | bytes 23085088 | tf_op jit(solution)/shard_map/sbmd,bcd->sbmc/dot_general | solution.py:81
  397.1 4.4 copy.76
  401.5 88.7 %all-to-all-start.1 = ((f32[32,8,32,128]{3,2,1,0:T(8,128)}), f32[32,8,32,128]{3,2,1,0:T(8,128)}, u32[]{:S(2)}, u32[]{:S(2)}) async-start(f32[32,8,32,128]{3,2,1,0:T(8,128)} %copy.76), calls=%async_computation.1 | async-start | bytes 8388608 | tf_op jit(solution)/shard_map/all_to_all | solution.py:91
  495.8 46.5 %all-to-all-done.1 = f32[32,8,32,128]{3,2,1,0:T(8,128)} async-done(((f32[32,8,32,128]{3,2,1,0:T(8,128)}), f32[32,8,32,128]{3,2,1,0:T(8,128)}, u32[]{:S(2)}, u32[]{:S(2)}) %all-to-all-start.1) | async-done | bytes 4194336 | tf_op jit(solution)/shard_map/all_to_all | solution.py:91
  542.3 13.0 %gather_fusion.1 = f32[4096,128]{1,0:T(8,128)S(1)} fusion(f32[8192,128]{1,0:T(8,128)} %bitcast.13, s32[4096]{0:T(1024)S(1)} %broadcast_clamp_fusion.3), kind=kCustom, calls=%fused_computation.1 | custom fusion | bytes 4210688 | tf_op jit(solution)/shard_map/gather | solution.py:94
  558.4 3.1 fusion.61
  561.5 28.0 %gather_fusion.4 = f32[8192,128]{1,0:T(8,128)} fusion(f32[4096,128]{1,0:T(8,128)S(1)} %get-tuple-element.7, s32[8192]{0:T(1024)S(1)} %broadcast_clamp_fusion), kind=kCustom, calls=%fused_computation.4 | custom fusion | bytes 8421376 | tf_op jit(solution)/shard_map/gather | solution.py:110
  589.4 5.2 broadcast_select_fusion
  594.7 7.4 all-to-all-start.3
  602.1 21.8 %fusion.21 = f32[8,32,32,128]{3,1,2,0:T(8,128)S(1)} fusion(bf16[8,2,128,1024]{3,2,1,0:T(8,128)(2,1)} %bitcast.101, bf16[32,8,32,1024]{3,2,1,0:T(8,128)(2,1)} %bitcast.85, pred[32,8,32]{0,2,1:T(8,128)(4,1)S(1)} %copy.74, pred[32,8,32]{0,2,1:T(8,128)(4,1)S(1)} %copy.73), kind=kOutput, calls=%fused_computation.41 | convolution fusion | flops 2164260864 | bytes 23085056 | tf_op jit(solution)/shard_map/sbmd,bcd->sbmc/dot_general | solution.py:86
  623.9 17.8 %fusion.12 = f32[32,8,32,128]{3,0,2,1:T(8,128)S(1)} fusion(f32[8,32,32,128]{3,1,2,0:T(8,128)S(1)} %fusion.21, bf16[8,2,128,1024]{3,2,1,0:T(8,128)(2,1)S(1)} %bitcast.102, pred[32,8,32]{0,2,1:T(8,128)(4,1)S(1)} %copy.82, pred[32,8,32]{0,2,1:T(8,128)(4,1)S(1)} %copy.80, bf16[32,8,32,1024]{3,2,1,0:T(8,128)(2,1)} %bitcast.86, pred[32,8,32]{0,2,1:T(8,128)(4,1)S(1)} %copy.74, ...), kind=kOutput, calls=%fused_computation.25 | convolution fusion | flops 2166358016 | bytes 27394048 | tf_op jit(solution)/shard_map/sbmd,bcd->sbmc/dot_general | solution.py:86
  641.8 4.4 copy.84
  646.2 7.8 all-to-all-done.3
  654.0 7.1 all-to-all-start.2
  661.2 4.6 copy.88
  666.5 22.2 %fusion.18 = f32[8,256,1024]{2,1,0:T(8,128)S(1)} fusion(bf16[32,8,32,128]{3,0,2,1:T(8,128)(2,1)S(1)} %get-tuple-element.4, bf16[32,8,32,128]{3,0,2,1:T(8,128)(2,1)S(1)} %get-tuple-element.5, bf16[32,8,32,1024]{3,2,1,0:T(8,128)(2,1)} %bitcast.87, pred[32,8,32]{0,2,1:T(8,128)(4,1)S(1)} %copy.74, pred[32,8,32]{0,2,1:T(8,128)(4,1)S(1)} %copy.73), kind=kOutput, calls=%fused_computation.37 | convolution fusion | flops 4320133120 | bytes 29376512 | tf_op jit(solution)/shard_map/sbmc,sbmd->bcd/dot_general | solution.py:122
  688.7 2.9 slice_add_fusion
  694.7 18.5 %all-to-all-done.2 = f32[32,8,32,128]{3,2,1,0:T(8,128)} async-done(((f32[32,8,32,128]{3,2,1,0:T(8,128)}), f32[32,8,32,128]{3,2,1,0:T(8,128)}, u32[]{:S(2)}, u32[]{:S(2)}) %all-to-all-start.2) | async-done | bytes 4194336 | tf_op jit(solution)/shard_map/all_to_all | solution.py:92
  713.2 16.5 %gather_fusion.3 = f32[4096,128]{1,0:T(8,128)} fusion(f32[8192,128]{1,0:T(8,128)} %bitcast.28, s32[4096]{0:T(1024)S(1)} %broadcast_clamp_fusion.3), kind=kCustom, calls=%fused_computation.3 | custom fusion | bytes 4210688 | tf_op jit(solution)/shard_map/gather | solution.py:97
  729.7 2.8 reshape.342
  733.3 4.4 bitcast_multiply_fusion
  740.2 12.3 %psum.15 = f32[1024]{0:T(1024)S(1)} all-reduce(f32[1024]{0:T(1024)S(1)} %bitcast.99), channel_id=1, replica_groups=mesh['dp'=4,'clus'=32] {'dp'}, use_global_device_ids=true, to_apply=%region_12.13 | all-reduce | flops 1024 | bytes 8192 | tf_op jit(solution)/shard_map/psum | solution.py:127
  752.6 36.4 %all-reduce.2.cloned.1.call-done = f32[1024,1024]{1,0:T(8,128)} async-done(((f32[1024,1024]{1,0:T(8,128)}), f32[1024,1024]{1,0:T(8,128)}) %all-reduce.2.cloned.1.call-update) | async-done | bytes 4194320 | tf_op jit(solution)/shard_map/psum | solution.py:127
  789.0 4.7 broadcast_divide_fusion
  (86 shorter events, 32.6 us)
Async XLA Ops:
  7.2 367.8 %copy-start = (bf16[1024,1024]{1,0:T(8,128)(2,1)S(1)}, bf16[1024,1024]{1,0:T(8,128)(2,1)}, u32[]{:S(2)}) copy-start(bf16[1024,1024]{1,0:T(8,128)(2,1)} %param.10) | copy-start | bytes 6291460
  7.2 127.6 %all-gather.2.cloned.1.call-start = ((), (), s32[]{:S(2)}) async-start(), calls=%async_computation.4 | async-start | bytes 34603008 | tf_op jit(solution)/shard_map/all_gather | solution.py:65
  9.5 51.3 %all-to-all-start = ((s32[32,512,8]{1,2,0:T(8,128)}), s32[32,512,8]{1,2,0:T(8,128)}, u32[]{:S(2)}, u32[]{:S(2)}) async-start(s32[32,512,8]{1,2,0:T(8,128)} %stack.2), calls=%async_computation | async-start | bytes 1048576 | tf_op jit(solution)/shard_map/all_to_all | solution.py:10
  134.8 240.2 %copy-start.8 = (f32[8]{0:T(128)S(1)}, f32[8]{0:T(128)}, u32[]{:S(2)}) copy-start(f32[8]{0:T(128)} %param.9) | copy-start | bytes 100
  401.5 88.7 %copy-start.5 = (s32[512,8]{0,1:T(8,128)S(1)}, s32[512,8]{0,1:T(8,128)}, u32[]{:S(2)}) copy-start(s32[512,8]{0,1:T(8,128)} %param.7) | copy-start | bytes 49156
  401.5 140.8 %all-to-all-start.1 = ((f32[32,8,32,128]{3,2,1,0:T(8,128)}), f32[32,8,32,128]{3,2,1,0:T(8,128)}, u32[]{:S(2)}, u32[]{:S(2)}) async-start(f32[32,8,32,128]{3,2,1,0:T(8,128)} %copy.76), calls=%async_computation.1 | async-start | bytes 8388608 | tf_op jit(solution)/shard_map/all_to_all | solution.py:91
  555.3 3.0 copy-start.2
  594.7 59.4 %all-to-all-start.3 = ((f32[32,256,128]{2,1,0:T(8,128)}), f32[32,256,128]{2,1,0:T(8,128)}, u32[]{:S(2)}, u32[]{:S(2)}) async-start(f32[32,256,128]{2,1,0:T(8,128)} %broadcast_select_fusion), calls=%async_computation.3 | async-start | bytes 8388608 | tf_op jit(solution)/shard_map/all_to_all | solution.py:111
  602.1 21.8 %copy-start.7 = (bf16[2048,1024]{1,0:T(8,128)(2,1)S(1)}, bf16[2048,1024]{1,0:T(8,128)(2,1)}, u32[]{:S(2)}) copy-start(bf16[2048,1024]{1,0:T(8,128)(2,1)} %param.11) | copy-start | bytes 12582916
  654.0 59.2 %all-to-all-start.2 = ((f32[32,8,32,128]{3,2,1,0:T(8,128)}), f32[32,8,32,128]{3,2,1,0:T(8,128)}, u32[]{:S(2)}, u32[]{:S(2)}) async-start(f32[32,8,32,128]{3,2,1,0:T(8,128)} %copy.84), calls=%async_computation.2 | async-start | bytes 8388608 | tf_op jit(solution)/shard_map/all_to_all | solution.py:92
  661.1 127.9 %all-reduce.2.cloned.1.call-start = ((), (), s32[]{:S(2)}) async-start(), calls=%async_computation.5 | async-start | bytes 8388608 | tf_op jit(solution)/shard_map/psum | solution.py:127
  691.6 1.6 copy-start.3
  729.7 3.6 copy-start.4
  752.6 41.1 %copy-start.6 = (f32[1024]{0:T(1024)}, f32[1024]{0:T(1024)S(1)}, u32[]{:S(2)}) copy-start(f32[1024]{0:T(1024)S(1)} %psum.15) | copy-start | bytes 12292
  752.6 41.1 %copy-start.1 = (bf16[1024,1024]{1,0:T(8,128)(2,1)S(1)}, bf16[1024,1024]{1,0:T(8,128)(2,1)}, u32[]{:S(2)}) copy-start(bf16[1024,1024]{1,0:T(8,128)(2,1)} %param.10) | copy-start | bytes 6291460
Sparse Core Ops, SparseCore 0:
  10.3 118.7 all-gather.1
  691.8 97.2 all-reduce.1
